TPU v7x, 32 devices: a whole 2x2x4 slice. The times are simulated.
32 devices in a mesh: dp: 2 (over y), row: 4 (over x, core), col: 4 (over z).
Axes of the slice: x: 2, y: 2, z: 4, core: 2. Of those that a mesh axis runs over, the one named last changes fastest.
Arguments:
- tokens: bfloat16 [1024, 1024], P(('dp', 'row'), 'col'), may hold values from -12 to 12
- cotangent: bfloat16 [1024, 1024], P(('dp', 'row'), 'col'), may hold values from -6 to 6
- first_gain: float32 [1024], P('col'), may hold values from 0.25 to 1.75
- first_shift: float32 [1024], P('col'), may hold values from -3 to 3
- w_qkv: bfloat16 [1024, 3072], P('col', 'row'), may hold values from -0.1875 to 0.1875
- bias_qv: float32 [2048], P('row'), may hold values from -4 to 4
- w_out: bfloat16 [1024, 1024], P('row', 'col'), may hold values from -0.375 to 0.375
- bias_out: float32 [1024], P('col'), may hold values from -3 to 3
- second_gain: float32 [1024], P('col'), may hold values from 0.25 to 1.75
- second_shift: float32 [1024], P('col'), may hold values from -3 to 3
- w_up: bfloat16 [1024, 4096], P('col', 'row'), may hold values from -0.1875 to 0.1875
- bias_up: float32 [4096], P('row'), may hold values from -4 to 4
- w_down: bfloat16 [4096, 1024], P('row', 'col'), may hold values from -0.125 to 0.125
- bias_down: float32 [1024], P('col'), may hold values from -3 to 3
Outputs:
- block_out: bfloat16 [1024, 1024], P(('dp', 'row'), 'col')
- grad_tokens: float32 [1024, 1024], P(('dp', 'row'), 'col')
- grad_first_gain: float32 [1024], P('col')
- grad_first_shift: float32 [1024], P('col')
- grad_w_qkv: float32 [1024, 3072], P('col', 'row')
- grad_bias_qv: float32 [2048], P('row')
- grad_w_out: float32 [1024, 1024], P('row', 'col')
- grad_bias_out: float32 [1024], P('col')
- grad_second_gain: float32 [1024], P('col')
- grad_second_shift: float32 [1024], P('col')
- grad_w_up: float32 [1024, 4096], P('col', 'row')
- grad_bias_up: float32 [4096], P('row')
- grad_w_down: float32 [4096, 1024], P('row', 'col')
- grad_bias_down: float32 [1024], P('col')
All inputs are finite; a program needn't handle non-finite values.
Results may differ from a plain program's by a relative error of at most 0.012.
Values may be sent and summed in bfloat16 or wider, within the bound.
No kernel may reach another device: no remote copies, remote signals or barrier semaphores. Data moves between devices by JAX's collectives and lax.ppermute only.
A program may use at most 64 MiB of HBM per device.

v0:
```python
import jax
import jax.numpy as jnp
from jax import lax
from jax.sharding import PartitionSpec as P

HEADS = 16
HEAD_DIM = 64
SEQ = 512
EPS = 1e-05
GELU_C = 0.7978845608028654
GELU_A = 0.044715


def gelu_pair(hidden):
    inner = GELU_C * (hidden + GELU_A * hidden * hidden * hidden)
    tanh_val = jnp.tanh(inner)
    value = 0.5 * hidden * (1.0 + tanh_val)
    slope = 0.5 * (1.0 + tanh_val) + 0.5 * hidden * (1.0 - tanh_val * tanh_val) * GELU_C * (
        1.0 + 3.0 * GELU_A * hidden * hidden
    )
    return (value, slope)


def feature_stats(first_part, second_part):
    return lax.psum((first_part, second_part), "col")


def normalize(matrix, gain, shift):
    width = matrix.shape[1] * lax.axis_size("col")
    total_one, total_two = feature_stats(jnp.sum(matrix, 1), jnp.sum(matrix * matrix, 1))
    centre = total_one / width
    spread = total_two / width - centre * centre
    rstd = lax.rsqrt(spread + EPS)[:, None]
    normed = (matrix - centre[:, None]) * rstd
    return (normed, rstd, (normed * gain + shift).astype(jnp.bfloat16))


def normalize_back(grad, normed, rstd, gain):
    width = grad.shape[1] * lax.axis_size("col")
    scaled = grad * gain
    total_one, total_two = feature_stats(jnp.sum(scaled, 1), jnp.sum(scaled * normed, 1))
    return rstd * (scaled - total_one[:, None] / width - normed * (total_two[:, None] / width))


def product(left, matrix, transposed):
    if transposed:
        return lax.dot_general(
            left, matrix, (((1,), (1,)), ((), ())), preferred_element_type=jnp.float32
        )
    return jnp.dot(left, matrix, preferred_element_type=jnp.float32)


def outer_grad(left, right):
    return lax.dot_general(
        left, right, (((0,), (0,)), ((), ())), preferred_element_type=jnp.float32
    )


def rows_in(block):
    return lax.all_gather(block, "row", axis=0, tiled=True)


def cols_in(block):
    return lax.all_gather(block, "col", axis=0, tiled=True)


def to_cols(whole, matrix, transposed):
    own_rows = whole.shape[0] // lax.axis_size("col")

    def term(first_row, row_count):
        return product(whole, matrix, transposed)

    return lax.psum_scatter(
        term(jnp.int32(0), lax.axis_size("col") * own_rows), "col", scatter_dimension=0, tiled=True
    )


def to_rows(whole, matrix, transposed):
    own_rows = whole.shape[0] // lax.axis_size("row")

    def term(first_row, row_count):
        return product(whole, matrix, transposed)

    return lax.psum_scatter(
        term(jnp.int32(0), lax.axis_size("row") * own_rows), "row", scatter_dimension=0, tiled=True
    )


def block_scores(query_block, query_pos, keys_all, slopes):
    key_pos = jnp.arange(keys_all.shape[0], dtype=jnp.int32)
    offsets = query_pos[:, None] - key_pos[None, :]
    causal_mask = (offsets >= 0) & (query_pos[:, None] // SEQ == key_pos[None, :] // SEQ)
    scores = (
        jnp.einsum("qhe,khe->hqk", query_block, keys_all, preferred_element_type=jnp.float32)
        * 0.125
    )
    scores = scores - slopes[:, None, None] * offsets.astype(jnp.float32)[None]
    return jnp.where(causal_mask[None], scores, -30000.0)


def local(
    tokens,
    cotangent,
    first_gain,
    first_shift,
    w_qkv,
    bias_qv,
    w_out,
    bias_out,
    second_gain,
    second_shift,
    w_up,
    bias_up,
    w_down,
    bias_down,
):
    rows_a = tokens.shape[0]
    group_rows = rows_a * lax.axis_size("row")
    rows_b = group_rows // lax.axis_size("col")
    head_count = bias_qv.shape[0] // (2 * HEAD_DIM)
    head_ids = lax.axis_index("row") * head_count + jnp.arange(head_count, dtype=jnp.int32)
    slopes = jnp.exp2(-8.0 * (head_ids.astype(jnp.float32) + 1.0) / HEADS)
    query_pos = lax.axis_index("col") * rows_b + jnp.arange(rows_b, dtype=jnp.int32)
    block_rows = min(rows_b, 512)
    block_count = rows_b // block_rows
    inputs_f = tokens.astype(jnp.float32)
    normed_one, rstd_one, first_in = normalize(inputs_f, first_gain, first_shift)
    first_all = rows_in(first_in)
    joined = to_cols(first_all, w_qkv, False).reshape(rows_b, head_count, 3, HEAD_DIM)
    bias_pair = bias_qv.reshape(head_count, 2, HEAD_DIM)
    queries = (joined[:, :, 0] + bias_pair[:, 0]).astype(jnp.bfloat16)
    keys_here = joined[:, :, 1].astype(jnp.bfloat16)
    values_here = (joined[:, :, 2] + bias_pair[:, 1]).astype(jnp.bfloat16)
    keys_flat, values_flat = (
        lax.all_gather(keys_here.reshape(rows_b, -1), "col", axis=0, tiled=True),
        lax.all_gather(values_here.reshape(rows_b, -1), "col", axis=0, tiled=True),
    )
    keys_all = keys_flat.reshape(group_rows, head_count, HEAD_DIM)
    values_all = values_flat.reshape(group_rows, head_count, HEAD_DIM)
    query_blocks = queries.reshape(block_count, block_rows, head_count, HEAD_DIM)
    pos_blocks = query_pos.reshape(block_count, block_rows)

    def forward_block(inputs):
        query_block, block_pos = inputs
        scores = block_scores(query_block, block_pos, keys_all, slopes)
        exponent = jnp.exp(scores)
        row_total = jnp.sum(exponent, -1)
        numerator = jnp.einsum(
            "hqk,khe->qhe",
            exponent.astype(jnp.bfloat16),
            values_all,
            preferred_element_type=jnp.float32,
        )
        context_block = (numerator / row_total.T[:, :, None]).astype(jnp.bfloat16)
        return (context_block, jnp.log(row_total))

    context_blocks, logsum_blocks = lax.map(forward_block, (query_blocks, pos_blocks))
    context = context_blocks.reshape(rows_b, head_count * HEAD_DIM)
    context_all = cols_in(context)
    resid = inputs_f + to_rows(context_all, w_out, False) + bias_out
    normed_two, rstd_two, second_in = normalize(resid, second_gain, second_shift)
    second_all = rows_in(second_in)
    pre_act = to_cols(second_all, w_up, False) + bias_up
    act, slope_act = gelu_pair(pre_act)
    act_all = cols_in(act.astype(jnp.bfloat16))
    block_out = (resid + to_rows(act_all, w_down, False) + bias_down).astype(jnp.bfloat16)
    cot_f = cotangent.astype(jnp.float32)
    cot_all = rows_in(cotangent)
    grad_down = outer_grad(act_all, cot_all)
    grad_pre = to_cols(cot_all, w_down, True) * slope_act
    up_bias_part = jnp.sum(grad_pre, 0)
    grad_pre_all = cols_in(grad_pre.astype(jnp.bfloat16))
    grad_up = outer_grad(second_all, grad_pre_all)
    grad_second = to_rows(grad_pre_all, w_up, True)
    second_gain_part = jnp.sum(grad_second * normed_two, 0)
    second_shift_part = jnp.sum(grad_second, 0)
    grad_resid = cot_f + normalize_back(grad_second, normed_two, rstd_two, second_gain)
    out_bias_part = jnp.sum(grad_resid, 0)
    down_bias_part = jnp.sum(cot_f, 0)
    resid_all = rows_in(grad_resid.astype(jnp.bfloat16))
    grad_out = outer_grad(context_all, resid_all)
    grad_context = to_cols(resid_all, w_out, True).astype(jnp.bfloat16)
    grad_ctx_blocks = grad_context.reshape(block_count, block_rows, head_count, HEAD_DIM)

    def backward_block(running, inputs):
        key_acc, value_acc = running
        query_block, block_pos, context_block, grad_block, logsum_block = inputs
        scores = block_scores(query_block, block_pos, keys_all, slopes)
        probs = jnp.exp(scores - logsum_block[:, :, None])
        delta = jnp.sum(grad_block.astype(jnp.float32) * context_block.astype(jnp.float32), -1).T
        dprob = jnp.einsum(
            "qhe,khe->hqk", grad_block, values_all, preferred_element_type=jnp.float32
        )
        dscore = (probs * (dprob - delta[:, :, None])).astype(jnp.bfloat16)
        grad_q = (
            jnp.einsum("hqk,khe->qhe", dscore, keys_all, preferred_element_type=jnp.float32) * 0.125
        )
        key_acc = (
            key_acc
            + jnp.einsum("hqk,qhe->khe", dscore, query_block, preferred_element_type=jnp.float32)
            * 0.125
        )
        value_acc = value_acc + jnp.einsum(
            "hqk,qhe->khe",
            probs.astype(jnp.bfloat16),
            grad_block,
            preferred_element_type=jnp.float32,
        )
        return ((key_acc, value_acc), grad_q)

    empty = jnp.zeros((group_rows, head_count, HEAD_DIM), jnp.float32)
    (key_acc, value_acc), grad_q_blocks = lax.scan(
        backward_block,
        (empty, empty),
        (query_blocks, pos_blocks, context_blocks, grad_ctx_blocks, logsum_blocks),
    )
    grad_k, grad_v = (
        lax.psum_scatter(key_acc.reshape(group_rows, -1), "col", scatter_dimension=0, tiled=True),
        lax.psum_scatter(value_acc.reshape(group_rows, -1), "col", scatter_dimension=0, tiled=True),
    )
    grad_q = grad_q_blocks.reshape(rows_b, head_count, HEAD_DIM)
    grad_k = grad_k.reshape(rows_b, head_count, HEAD_DIM)
    grad_v = grad_v.reshape(rows_b, head_count, HEAD_DIM)
    grad_joined = jnp.stack([grad_q, grad_k, grad_v], 2)
    qv_bias_part = jnp.sum(jnp.stack([grad_q, grad_v], 2), 0).reshape(-1)
    joined_all = cols_in(grad_joined.reshape(rows_b, -1).astype(jnp.bfloat16))
    grad_qkv = outer_grad(first_all, joined_all)
    grad_first = to_rows(joined_all, w_qkv, True)
    first_gain_part = jnp.sum(grad_first * normed_one, 0)
    first_shift_part = jnp.sum(grad_first, 0)
    grad_tokens = grad_resid + normalize_back(grad_first, normed_one, rstd_one, first_gain)
    grad_qkv, grad_out, grad_up, grad_down = lax.psum(
        (grad_qkv, grad_out, grad_up, grad_down), "dp"
    )
    gain_one, shift_one, gain_two, shift_two, out_bias_grad, down_bias_grad = lax.psum(
        (
            first_gain_part,
            first_shift_part,
            second_gain_part,
            second_shift_part,
            out_bias_part,
            down_bias_part,
        ),
        ("dp", "row"),
    )
    qv_bias_grad, up_bias_grad = lax.psum((qv_bias_part, up_bias_part), ("dp", "col"))
    return (
        block_out,
        grad_tokens,
        gain_one,
        shift_one,
        grad_qkv,
        qv_bias_grad,
        grad_out,
        out_bias_grad,
        gain_two,
        shift_two,
        grad_up,
        up_bias_grad,
        grad_down,
        down_bias_grad,
    )


def solution(mesh):
    placed = (
        P(("dp", "row"), "col"),
        P(("dp", "row"), "col"),
        P("col"),
        P("col"),
        P("col", "row"),
        P("row"),
        P("row", "col"),
        P("col"),
        P("col"),
        P("col"),
        P("col", "row"),
        P("row"),
        P("row", "col"),
        P("col"),
    )
    return jax.shard_map(
        local,
        mesh=mesh,
        in_specs=placed,
        out_specs=(
            P(("dp", "row"), "col"),
            P(("dp", "row"), "col"),
            P("col"),
            P("col"),
            P("col", "row"),
            P("row"),
            P("row", "col"),
            P("col"),
            P("col"),
            P("col"),
            P("col", "row"),
            P("row"),
            P("row", "col"),
            P("col"),
        ),
        check_vma=False,
    )
```

profile of v0, /device:TPU:0, one launch (start us, length us, event | category | flops | bytes accessed | tf_op | source)
XLA Modules:
  0.0 548.3 jit_solution(9419298570931146965)
XLA Ops:
  7.2 1.0 convert_reduce_fusion
  8.2 13.5 %all-reduce.5 = (f32[128]{0:T(128)S(1)}, f32[128]{0:T(128)S(1)}) all-reduce(f32[128]{0:T(128)S(1)} %get-tuple-element.85, f32[128]{0:T(128)S(1)} %get-tuple-element.84), channel_id=1, replica_groups=mesh['dp'=2,'row'=4,'col'=4] {'col'}, use_global_device_ids=true, to_apply=%region_3.0 | all-reduce | flops 256 | bytes 2048 | tf_op jit(solution)/shard_map/psum | solution.py:25
  21.7 1.0 fusion.26
  22.7 5.8 %all_gather.30 = bf16[512,256]{1,0:T(8,128)(2,1)S(1)} all-gather(bf16[128,256]{1,0:T(8,128)(2,1)S(1)} %fusion.26), channel_id=1, replica_groups=mesh['dp'=2,'row'=4,'col'=4] {'row'}, dimensions={0}, use_global_device_ids=true | all-gather | bytes 327680 | tf_op jit(solution)/shard_map/all_gather | solution.py:60
  28.5 0.7 copy-done.3
  29.2 2.5 fusion.49
  32.3 33.3 %reduce-scatter.11.cloned.1.call-done = f32[128,768]{1,0:T(8,128)} async-done(((f32[512,768]{1,0:T(8,128)}), f32[128,768]{1,0:T(8,128)}) %reduce-scatter.11.cloned.1.call-update) | async-done | bytes 393232 | tf_op jit(solution)/shard_map/reduce_scatter | solution.py:73
  65.6 1.1 copy.38
  66.9 13.4 %all_gather.31 = bf16[512,256]{0,1:T(8,128)(2,1)S(1)} all-gather(bf16[128,256]{0,1:T(8,128)(2,1)S(1)} %fusion.36), channel_id=1, replica_groups=mesh['dp'=2,'row'=4,'col'=4] {'col'}, dimensions={0}, use_global_device_ids=true | all-gather | bytes 327680 | tf_op jit(solution)/shard_map/all_gather | solution.py:136
  80.2 13.2 %all_gather.32 = bf16[512,256]{0,1:T(8,128)(2,1)S(1)} all-gather(bf16[128,256]{0,1:T(8,128)(2,1)S(1)} %bitcast.91), channel_id=1, replica_groups=mesh['dp'=2,'row'=4,'col'=4] {'col'}, dimensions={0}, use_global_device_ids=true | all-gather | bytes 327680 | tf_op jit(solution)/shard_map/all_gather | solution.py:135
  93.5 0.7 exponential_reduce_fusion
  94.5 12.8 %all_gather.33 = bf16[512,256]{0,1:T(8,128)(2,1)S(1)} all-gather(bf16[128,256]{0,1:T(8,128)(2,1)S(1)} %bitcast.89), channel_id=1, replica_groups=mesh['dp'=2,'row'=4,'col'=4] {'col'}, dimensions={0}, use_global_device_ids=true | all-gather | bytes 327680 | tf_op jit(solution)/shard_map/all_gather | solution.py:64
  107.3 0.7 copy-done.5
  108.0 1.1 fusion.50
  109.1 5.8 %all_gather.36 = bf16[512,256]{1,0:T(8,128)(2,1)S(1)} all-gather(bf16[128,256]{1,0:T(8,128)(2,1)S(1)} %copy-done.21), channel_id=1, replica_groups=mesh['dp'=2,'row'=4,'col'=4] {'row'}, dimensions={0}, use_global_device_ids=true | all-gather | bytes 327680 | tf_op jit(solution)/shard_map/all_gather | solution.py:60
  114.9 0.7 copy-done.9
  115.7 1.8 fusion.53
  117.6 11.7 %reduce-scatter.13.cloned.1.call-done = f32[128,256]{1,0:T(8,128)} async-done(((f32[512,256]{1,0:T(8,128)}), f32[128,256]{1,0:T(8,128)}) %reduce-scatter.13.cloned.1.call-update) | async-done | bytes 131088 | tf_op jit(solution)/shard_map/reduce_scatter | solution.py:84
  129.2 1.0 fusion.42
  130.2 11.8 %all-reduce.4 = (f32[128]{0:T(128)S(1)}, f32[128]{0:T(128)S(1)}) all-reduce(f32[128]{0:T(128)S(1)} %get-tuple-element.83, f32[128]{0:T(128)S(1)} %get-tuple-element.82), channel_id=1, replica_groups=mesh['dp'=2,'row'=4,'col'=4] {'col'}, use_global_device_ids=true, to_apply=%region_10.11 | all-reduce | flops 256 | bytes 2048 | tf_op jit(solution)/shard_map/psum | solution.py:25
  142.2 5.8 %all_gather.34 = bf16[512,256]{1,0:T(8,128)(2,1)S(1)} all-gather(bf16[128,256]{1,0:T(8,128)(2,1)S(1)} %add_convert_fusion.1), channel_id=1, replica_groups=mesh['dp'=2,'row'=4,'col'=4] {'row'}, dimensions={0}, use_global_device_ids=true | all-gather | bytes 327680 | tf_op jit(solution)/shard_map/all_gather | solution.py:60
  148.0 0.7 copy-done.11
  148.7 1.7 fusion.51
  150.5 24.8 %reduce-scatter.19.cloned.1.call-done = f32[128,1024]{1,0:T(8,128)} async-done(((f32[512,1024]{1,0:T(8,128)}), f32[128,1024]{1,0:T(8,128)}) %reduce-scatter.19.cloned.1.call-update) | async-done | bytes 524304 | tf_op jit(solution)/shard_map/reduce_scatter | solution.py:73
  175.2 44.9 %reduce-scatter.15.cloned.1.call-done = f32[128,1024]{1,0:T(8,128)} async-done(((f32[512,1024]{1,0:T(8,128)}), f32[128,1024]{1,0:T(8,128)}) %reduce-scatter.15.cloned.1.call-update) | async-done | bytes 524304 | tf_op jit(solution)/shard_map/reduce_scatter | solution.py:73
  220.1 2.4 fusion.43
  222.6 0.5 all-gather.3.cloned.1.call-update
  223.2 26.7 %all-gather.5.cloned.1.call-done = bf16[512,1024]{1,0:T(8,128)(2,1)} async-done(((bf16[128,1024]{1,0:T(8,128)(2,1)}), bf16[512,1024]{1,0:T(8,128)(2,1)}) %all-gather.5.cloned.1.call-update) | async-done | bytes 1048592 | tf_op jit(solution)/shard_map/all_gather | solution.py:64
  249.9 2.5 fusion.54
  252.5 26.8 %all-gather.3.cloned.1.call-done = bf16[512,1024]{1,0:T(8,128)(2,1)} async-done(((bf16[128,1024]{1,0:T(8,128)(2,1)}), bf16[512,1024]{1,0:T(8,128)(2,1)}) %all-gather.3.cloned.1.call-update) | async-done | bytes 1048592 | tf_op jit(solution)/shard_map/all_gather | solution.py:64
  279.3 2.5 fusion.52
  281.8 21.6 %reduce-scatter.21.cloned.1.call-done = f32[128,256]{1,0:T(8,128)} async-done(((f32[512,256]{1,0:T(8,128)}), f32[128,256]{1,0:T(8,128)}) %reduce-scatter.21.cloned.1.call-update) | async-done | bytes 131088 | tf_op jit(solution)/shard_map/reduce_scatter | solution.py:84
  303.4 1.1 multiply_reduce_fusion
  304.5 11.7 %all-reduce.3 = (f32[128]{0:T(128)S(1)}, f32[128]{0:T(128)S(1)}) all-reduce(f32[128]{0:T(128)S(1)} %get-tuple-element.63, f32[128]{0:T(128)S(1)} %get-tuple-element.67), channel_id=1, replica_groups=mesh['dp'=2,'row'=4,'col'=4] {'col'}, use_global_device_ids=true, to_apply=%region_18.19 | all-reduce | flops 256 | bytes 2048 | tf_op jit(solution)/shard_map/psum | solution.py:25
  316.2 12.0 %reduce-scatter.17.cloned.1.call-done = f32[128,256]{1,0:T(8,128)} async-done(((f32[512,256]{1,0:T(8,128)}), f32[128,256]{1,0:T(8,128)}) %reduce-scatter.17.cloned.1.call-update) | async-done | bytes 131088 | tf_op jit(solution)/shard_map/reduce_scatter | solution.py:84
  328.1 1.6 fusion.45
  329.8 5.8 %all_gather.38 = bf16[512,256]{1,0:T(8,128)(2,1)S(1)} all-gather(bf16[128,256]{1,0:T(8,128)(2,1)S(1)} %convert_element_type.98), channel_id=1, replica_groups=mesh['dp'=2,'row'=4,'col'=4] {'row'}, dimensions={0}, use_global_device_ids=true | all-gather | bytes 327680 | tf_op jit(solution)/shard_map/all_gather | solution.py:60
  335.6 0.7 copy-done.7
  336.3 1.1 fusion.55
  337.4 21.9 %reduce-scatter.23.cloned.1.call-done = f32[128,256]{1,0:T(8,128)} async-done(((f32[512,256]{1,0:T(8,128)}), f32[128,256]{1,0:T(8,128)}) %reduce-scatter.23.cloned.1.call-update) | async-done | bytes 131088 | tf_op jit(solution)/shard_map/reduce_scatter | solution.py:73
  359.3 0.9 convert_element_type.99
  360.3 1.2 fusion.14
  362.0 1.1 convolution_multiply_fusion.1
  363.2 0.9 fusion.48
  364.1 18.0 %reduce-scatter.27.cloned.1.call-done = f32[128,256]{0,1:T(8,128)} async-done(((f32[512,256]{0,1:T(8,128)}), f32[128,256]{0,1:T(8,128)}) %reduce-scatter.27.cloned.1.call-update) | async-done | bytes 131088 | tf_op jit(solution)/shard_map/reduce_scatter | solution.py:219
  382.1 0.9 bitcast_convert_fusion
  383.0 22.0 %reduce-scatter.25.cloned.1.call-done = f32[128,256]{0,1:T(8,128)} async-done(((f32[512,256]{0,1:T(8,128)}), f32[128,256]{0,1:T(8,128)}) %reduce-scatter.25.cloned.1.call-update) | async-done | bytes 131088 | tf_op jit(solution)/shard_map/reduce_scatter | solution.py:218
  405.0 0.9 convert.15
  405.9 17.0 %all_gather.39 = bf16[512,768]{0,1:T(8,128)(2,1)S(1)} all-gather(bf16[128,768]{0,1:T(8,128)(2,1)S(1)} %bitcast.88), channel_id=1, replica_groups=mesh['dp'=2,'row'=4,'col'=4] {'col'}, dimensions={0}, use_global_device_ids=true | all-gather | bytes 983040 | tf_op jit(solution)/shard_map/all_gather | solution.py:64
  422.9 2.3 fusion.56
  425.3 2.4 fusion.59
  427.8 1.4 fusion.60
  429.3 0.9 fusion.58
  430.2 1.3 fusion.57
  431.8 20.6 %all-reduce = (f32[512]{0:T(512)}, f32[1024]{0:T(1024)}) all-reduce(f32[512]{0:T(512)S(1)} %reshape.258, f32[1024]{0:T(1024)S(1)} %get-tuple-element.106), channel_id=1, replica_groups=mesh['dp'=2,'row'=4,'col'=4] {'dp','col'}, use_global_device_ids=true, to_apply=%region_34.35 | all-reduce | flops 1536 | bytes 12288 | tf_op jit(solution)/shard_map/psum | solution.py:246
  452.3 1.1 fusion.31
  453.4 8.4 %all-reduce.2 = (f32[128]{0:T(128)S(1)}, f32[128]{0:T(128)S(1)}) all-reduce(f32[128]{0:T(128)S(1)} %get-tuple-element.65, f32[128]{0:T(128)S(1)} %get-tuple-element.66), channel_id=1, replica_groups=mesh['dp'=2,'row'=4,'col'=4] {'col'}, use_global_device_ids=true, to_apply=%region_27.28 | all-reduce | flops 256 | bytes 2048 | tf_op jit(solution)/shard_map/psum | solution.py:25
  461.8 13.0 %all-reduce.1 = (f32[256]{0:T(256)}, f32[256]{0:T(256)}, f32[256]{0:T(256)}, f32[256]{0:T(256)}, f32[256]{0:T(256)}, /*index=5*/f32[256]{0:T(256)}) all-reduce(f32[256]{0:T(256)S(1)} %get-tuple-element.64, f32[256]{0:T(256)S(1)} %get-tuple-element.81, ...), channel_id=1, replica_groups=mesh['dp'=2,'row'=4,'col'=4] {'dp','row'}, use_global_device_ids=true, to_apply=%region_29.30 | all-reduce | flops 1536 | bytes 12288 | tf_op jit(solution)/shard_map/psum | solution.py:235
  474.8 1.7 fusion.30
  476.5 59.5 %all-reduce.9.cloned.1.call-done = (f32[256,768]{1,0:T(8,128)}, f32[256,256]{1,0:T(8,128)}, f32[256,1024]{1,0:T(8,128)}, f32[1024,256]{1,0:T(8,128)}) async-done(((f32[256,768]{1,0:T(8,128)}, f32[256,256]{1,0:T(8,128)}, f32[256,1024]{1,0:T(8,128)}, f32[1024,256]{1,0:T(8,128)}), (f32[256,768]{1,0:T(8,128)}, f32[256,256]{1,0:T(8,128)}, f32[256,1024]{1,0:T(8,128)}, ...) | async-done | bytes 3145744 | tf_op jit(solution)/shard_map/psum | solution.py:232
  536.0 2.2 copy.46
  538.2 1.7 copy.47
  539.9 1.0 copy.48
  540.8 1.0 copy.49
  (108 shorter events, 2.7 us)
Async XLA Ops:
  7.2 141.5 %copy-start = (bf16[256,1024]{1,0:T(8,128)(2,1)S(1)}, bf16[256,1024]{1,0:T(8,128)(2,1)}, u32[]{:S(2)}) copy-start(bf16[256,1024]{1,0:T(8,128)(2,1)} %param.24) | copy-start | bytes 1572868
  7.2 58.4 %reduce-scatter.11.cloned.1.call-start = ((), (), s32[]{:S(2)}) async-start(), calls=%async_computation.10 | async-start | bytes 1966080 | tf_op jit(solution)/shard_map/reduce_scatter | solution.py:73
  22.7 9.1 %copy-start.25 = (f32[512]{0:T(512)S(1)}, f32[512]{0:T(512)}, u32[]{:S(2)}) copy-start(f32[512]{0:T(512)} %param.19) | copy-start | bytes 6148
  28.5 0.7 copy-start.3
  31.8 97.5 %reduce-scatter.13.cloned.1.call-start = ((), (), s32[]{:S(2)}) async-start(), calls=%async_computation.11 | async-start | bytes 655360 | tf_op jit(solution)/shard_map/reduce_scatter | solution.py:84
  80.2 27.8 %copy-start.18 = (bf16[256,256]{1,0:T(8,128)(2,1)S(1)}, bf16[256,256]{1,0:T(8,128)(2,1)}, u32[]{:S(2)}) copy-start(bf16[256,256]{1,0:T(8,128)(2,1)} %param.20) | copy-start | bytes 393220
  94.2 15.0 %copy-start.21 = (bf16[128,256]{1,0:T(8,128)(2,1)S(1)}, bf16[128,256]{1,0:T(8,128)(2,1)}, u32[]{:S(2)}) copy-start(bf16[128,256]{1,0:T(8,128)(2,1)} %param.15) | copy-start | bytes 196612
  94.2 21.5 %copy-start.12 = (bf16[1024,256]{1,0:T(8,128)(2,1)S(1)}, bf16[1024,256]{1,0:T(8,128)(2,1)}, u32[]{:S(2)}) copy-start(bf16[1024,256]{1,0:T(8,128)(2,1)} %param.26) | copy-start | bytes 1572868
  107.3 0.7 copy-start.5
  109.1 66.1 %reduce-scatter.19.cloned.1.call-start = ((), (), s32[]{:S(2)}) async-start(), calls=%async_computation.15 | async-start | bytes 2621440 | tf_op jit(solution)/shard_map/reduce_scatter | solution.py:73
  114.9 0.7 copy-start.9
  115.6 13.6 %copy-start.13 = (bf16[128,256]{1,0:T(8,128)(2,1)S(1)}, bf16[128,256]{1,0:T(8,128)(2,1)}, u32[]{:S(2)}) copy-start(bf16[128,256]{1,0:T(8,128)(2,1)} %param.14) | copy-start | bytes 196612
  115.6 13.6 %copy-start.26 = (f32[256]{0:T(256)S(1)}, f32[256]{0:T(256)}, u32[]{:S(2)}) copy-start(f32[256]{0:T(256)} %param.21) | copy-start | bytes 3076
  115.6 26.4 %copy-start.22 = (f32[256]{0:T(256)S(1)}, f32[256]{0:T(256)}, u32[]{:S(2)}) copy-start(f32[256]{0:T(256)} %param.22) | copy-start | bytes 3076
  115.6 26.4 %copy-start.27 = (f32[256]{0:T(256)S(1)}, f32[256]{0:T(256)}, u32[]{:S(2)}) copy-start(f32[256]{0:T(256)} %param.23) | copy-start | bytes 3076
  117.5 102.6 %reduce-scatter.15.cloned.1.call-start = ((), (), s32[]{:S(2)}) async-start(), calls=%async_computation.12 | async-start | bytes 2621440 | tf_op jit(solution)/shard_map/reduce_scatter | solution.py:73
  148.0 0.7 copy-start.11
  148.7 71.5 %copy-start.24 = (f32[1024]{0:T(1024)S(1)}, f32[1024]{0:T(1024)}, u32[]{:S(2)}) copy-start(f32[1024]{0:T(1024)} %param.25) | copy-start | bytes 12292
  150.4 99.5 %all-gather.5.cloned.1.call-start = ((), (), s32[]{:S(2)}) async-start(), calls=%async_computation.16 | async-start | bytes 1310720 | tf_op jit(solution)/shard_map/all_gather | solution.py:64
  222.5 56.7 %all-gather.3.cloned.1.call-start = ((), (), s32[]{:S(2)}) async-start(), calls=%async_computation.13 | async-start | bytes 1310720 | tf_op jit(solution)/shard_map/all_gather | solution.py:64
  223.1 80.2 %reduce-scatter.21.cloned.1.call-start = ((), (), s32[]{:S(2)}) async-start(), calls=%async_computation.17 | async-start | bytes 655360 | tf_op jit(solution)/shard_map/reduce_scatter | solution.py:84
  252.4 75.7 %copy-start.28 = (f32[256]{0:T(256)S(1)}, f32[256]{0:T(256)}, u32[]{:S(2)}) copy-start(f32[256]{0:T(256)} %param.27) | copy-start | bytes 3076
  252.4 75.7 %reduce-scatter.17.cloned.1.call-start = ((), (), s32[]{:S(2)}) async-start(), calls=%async_computation.14 | async-start | bytes 655360 | tf_op jit(solution)/shard_map/reduce_scatter | solution.py:84
  281.8 77.6 %reduce-scatter.23.cloned.1.call-start = ((), (), s32[]{:S(2)}) async-start(), calls=%async_computation.18 | async-start | bytes 655360 | tf_op jit(solution)/shard_map/reduce_scatter | solution.py:73
  329.8 31.8 %copy-start.14 = (f32[128,256]{1,0:T(8,128)}, f32[128,256]{1,0:T(8,128)S(1)}, u32[]{:S(2)}) copy-start(f32[128,256]{1,0:T(8,128)S(1)} %get-tuple-element.109) | copy-start | bytes 393220
  335.5 0.7 copy-start.7
  337.3 44.7 %reduce-scatter.27.cloned.1.call-start = ((), (), s32[]{:S(2)}) async-start(), calls=%async_computation.20 | async-start | bytes 655360 | tf_op jit(solution)/shard_map/reduce_scatter | solution.py:219
  361.5 43.4 %reduce-scatter.25.cloned.1.call-start = ((), (), s32[]{:S(2)}) async-start(), calls=%async_computation.19 | async-start | bytes 655360 | tf_op jit(solution)/shard_map/reduce_scatter | solution.py:218
  363.1 89.2 %reduce-scatter.29.cloned.1.call-start = ((), (), s32[]{:S(2)}) async-start(), calls=%async_computation.21 | async-start | bytes 655360 | tf_op jit(solution)/shard_map/reduce_scatter | solution.py:84
  383.0 42.3 %copy-start.1 = (bf16[512,1024]{1,0:T(8,128)(2,1)S(1)}, bf16[512,1024]{1,0:T(8,128)(2,1)}, u32[]{:S(2)}) copy-start(bf16[512,1024]{1,0:T(8,128)(2,1)} %all-gather.5.cloned.1.call-done) | copy-start | bytes 3145732
  422.9 4.9 copy-start.2
  425.3 110.7 %all-reduce.9.cloned.1.call-start = ((), (), s32[]{:S(2)}) async-start(), calls=%async_computation.22 | async-start | bytes 6291456 | tf_op jit(solution)/shard_map/psum | solution.py:232
  425.3 2.5 copy-start.10
  425.3 3.9 copy-start.6
  425.3 3.9 copy-start.8
  427.8 2.4 copy-start.4
  430.2 1.3 copy-start.19
  430.2 1.3 copy-start.20
  431.5 20.9 %copy-start.23 = (f32[256]{0:T(256)S(1)}, f32[256]{0:T(256)}, u32[]{:S(2)}) copy-start(f32[256]{0:T(256)} %param.16) | copy-start | bytes 3076
  431.5 43.3 %copy-start.15 = (f32[128,256]{1,0:T(8,128)S(1)}, f32[128,256]{1,0:T(8,128)}, u32[]{:S(2)}) copy-start(f32[128,256]{1,0:T(8,128)} %copy-done.14) | copy-start | bytes 393220
  536.0 3.9 copy-start.17
  536.0 4.9 copy-start.16
Sparse Core Ops, SparseCore 0:
  31.9 33.6 reduce-scatter.10
  109.2 19.9 reduce-scatter.12
  131.5 43.6 reduce-scatter.18
  177.4 42.6 reduce-scatter.14
  222.7 27.1 all-gather.4
  251.9 27.3 all-gather.2
  282.3 20.9 reduce-scatter.20
  306.4 21.6 reduce-scatter.16
  337.5 21.8 reduce-scatter.22
  362.0 20.0 reduce-scatter.26
  384.9 20.0 reduce-scatter.24
  425.4 20.7 reduce-scatter.28
  449.8 86.1 all-reduce.8
where the time goes:
time: 549 us; the launch traced here: 548 us
  waiting for transfers between devices  324 us (59%)
  blocking collectives  158 us (29%)
  matrix products  26.1 us (5%)
  other arithmetic  14.3 us (3%)
  between operations  14.2 us (3%)
  local copies, waits for them, and re-layouts  11 us (2%)
    reduce_scatter x4, waiting for transfers between devices, to_cols(): lax.psum_scatter(term(jnp.int32(0), lax.axis_size('col') * own_rows), 'co...  125 us
    psum x1, waiting for transfers between devices, local(): lax.psum((grad_qkv, grad_out, grad_up, grad_down), 'dp')  59.5 us
    all_gather x2, waiting for transfers between devices, cols_in(): return lax.all_gather(block, 'col', axis=0, tiled=True)  53.5 us
    psum x4, blocking collectives, feature_stats(): return lax.psum((first_part, second_part), 'col')  45.4 us
    reduce_scatter x4, waiting for transfers between devices, to_rows(): lax.psum_scatter(term(jnp.int32(0), lax.axis_size('row') * own_rows), 'ro...  45.2 us
    all_gather x2, blocking collectives, cols_in(): return lax.all_gather(block, 'col', axis=0, tiled=True)  29.8 us
    all_gather x4, blocking collectives, rows_in(): return lax.all_gather(block, 'row', axis=0, tiled=True)  23.1 us
    reduce_scatter x1, waiting for transfers between devices, local(): lax.psum_scatter(key_acc.reshape(group_rows, -1), 'col', scatter_dimensio...  22 us
  transfers between devices with their start and end apart: 13, of which 12 were waited for; matrix products, arithmetic and copies ran while one was open for 4% of the time, Pallas kernels for 0%

commit v1 on v0

--- a/solution.py
+++ b/solution.py
@@ -9,6 +9,19 @@
 EPS = 1e-05
 GELU_C = 0.7978845608028654
 GELU_A = 0.044715
+
+
+def collect(shard, axis, dim):
+    ways = lax.axis_size(axis)
+    up = [(d, (d + 1) % ways) for d in range(ways)]
+    down = [(d, (d - 1) % ways) for d in range(ways)]
+    earlier, later = ([shard], [shard])
+    for _ in range(ways // 2):
+        earlier.append(lax.ppermute(earlier[-1], axis, up))
+    for _ in range((ways - 1) // 2):
+        later.append(lax.ppermute(later[-1], axis, down))
+    line = jnp.concatenate([*earlier[::-1], *later[1:]], axis=dim)
+    return jnp.roll(line, (lax.axis_index(axis) - ways // 2) * shard.shape[dim], axis=dim)
 
 
 def gelu_pair(hidden):
@@ -61,7 +74,7 @@
 
 
 def cols_in(block):
-    return lax.all_gather(block, "col", axis=0, tiled=True)
+    return collect(block, "col", 0)
 
 
 def to_cols(whole, matrix, transposed):

time: 549 us -> 524 us (0.954)
  blocking collectives: 158 us -> 130 us
  waiting for transfers between devices: 324 us -> 296 us
  starting transfers between devices: 0.54 us -> 19.1 us
  other arithmetic: 14.3 us -> 23.9 us
    all_gather x2 -> x0, waiting for transfers between devices: 53.5 us -> none  [cols_in(): return lax.all_gather(block, 'col', axis=0, tiled=True)]
    ppermute x0 -> x12, waiting for transfers between devices: none -> 42.9 us  [the longest x8 33.4 us: collect(): earlier.append(lax.ppermute(earlier[-1], axis, up))]
    all_gather x2 -> x0, blocking collectives: 29.8 us -> none  [cols_in(): return lax.all_gather(block, 'col', axis=0, tiled=True)]
    ppermute x0 -> x12, starting transfers between devices: none -> 18.7 us  [the longest x4 12.6 us: collect(): later.append(lax.ppermute(later[-1], axis, down))]
    reduce_scatter x4, waiting for transfers between devices: 45.2 us -> 28 us  [to_rows(): lax.psum_scatter(term(jnp.int32(0), lax.axis_size('row') * own_rows), 'ro...]
    concatenate x0 -> x2, other arithmetic: none -> 8.45 us  [collect(): jnp.roll(line, (lax.axis_index(axis) - ways // 2) * shard.shape[dim], axi...]
    unnamed x62 -> x112, local copies, waits for them, and re-layouts: 9.46 us -> 13.2 us
  transfers between devices with their start and end apart: 13 -> 23, of which waited for: 12 -> 18; matrix products, arithmetic and copies ran while one was open for 4% -> 6% of each run, Pallas kernels for 0% -> 0%
where the time goes in v1:
time: 524 us; the launch traced here: 523 us
  waiting for transfers between devices  296 us (56%)
  blocking collectives  130 us (25%)
  matrix products  25.4 us (5%)
  other arithmetic  23.9 us (5%)
  starting transfers between devices  19.1 us (4%)
  local copies, waits for them, and re-layouts  14.9 us (3%)
  between operations  14.6 us (3%)
    reduce_scatter x4, waiting for transfers between devices, to_cols(): lax.psum_scatter(term(jnp.int32(0), lax.axis_size('col') * own_rows), 'co...  125 us
    psum x1, waiting for transfers between devices, local(): lax.psum((grad_qkv, grad_out, grad_up, grad_down), 'dp')  60.4 us
    psum x4, blocking collectives, feature_stats(): return lax.psum((first_part, second_part), 'col')  45.3 us
    ppermute x8, waiting for transfers between devices, collect(): earlier.append(lax.ppermute(earlier[-1], axis, up))  33.4 us
    reduce_scatter x4, waiting for transfers between devices, to_rows(): lax.psum_scatter(term(jnp.int32(0), lax.axis_size('row') * own_rows), 'ro...  28 us
    all_gather x4, blocking collectives, rows_in(): return lax.all_gather(block, 'row', axis=0, tiled=True)  23.1 us
    reduce_scatter x1, waiting for transfers between devices, local(): lax.psum_scatter(value_acc.reshape(group_rows, -1), 'col', scatter_dimens...  22.1 us
    psum x1, blocking collectives, local(): lax.psum((qv_bias_part, up_bias_part), ('dp', 'col'))  21.9 us
  transfers between devices with their start and end apart: 23, of which 18 were waited for; matrix products, arithmetic and copies ran while one was open for 6% of the time, Pallas kernels for 0%

profile of v1, /device:TPU:0, one launch (start us, length us, event | category | flops | bytes accessed | tf_op | source)
XLA Modules:
  0.0 523.5 jit_solution(12590062027215117059)
XLA Ops:
  7.2 1.0 convert_reduce_fusion
  8.2 13.5 %all-reduce.5 = (f32[128]{0:T(128)S(1)}, f32[128]{0:T(128)S(1)}) all-reduce(f32[128]{0:T(128)S(1)} %get-tuple-element.86, f32[128]{0:T(128)S(1)} %get-tuple-element.85), channel_id=1, replica_groups=mesh['dp'=2,'row'=4,'col'=4] {'col'}, use_global_device_ids=true, to_apply=%region_3.0 | all-reduce | flops 256 | bytes 2048 | tf_op jit(solution)/shard_map/psum | solution.py:38
  22.7 5.8 %all_gather.18 = bf16[512,256]{1,0:T(8,128)(2,1)S(1)} all-gather(bf16[128,256]{1,0:T(8,128)(2,1)S(1)} %fusion.48), channel_id=1, replica_groups=mesh['dp'=2,'row'=4,'col'=4] {'row'}, dimensions={0}, use_global_device_ids=true | all-gather | bytes 327680 | tf_op jit(solution)/shard_map/all_gather | solution.py:73
  28.5 2.5 fusion.75
  31.6 33.3 %reduce-scatter.11.cloned.1.call-done = f32[128,768]{1,0:T(8,128)} async-done(((f32[512,768]{1,0:T(8,128)}), f32[128,768]{1,0:T(8,128)}) %reduce-scatter.11.cloned.1.call-update) | async-done | bytes 393232 | tf_op jit(solution)/shard_map/reduce_scatter | solution.py:86
  64.9 1.1 copy.38
  66.2 13.4 %all_gather.19 = bf16[512,256]{0,1:T(8,128)(2,1)S(1)} all-gather(bf16[128,256]{0,1:T(8,128)(2,1)S(1)} %fusion.58), channel_id=1, replica_groups=mesh['dp'=2,'row'=4,'col'=4] {'col'}, dimensions={0}, use_global_device_ids=true | all-gather | bytes 327680 | tf_op jit(solution)/shard_map/all_gather | solution.py:149
  79.6 13.1 %all_gather.20 = bf16[512,256]{0,1:T(8,128)(2,1)S(1)} all-gather(bf16[128,256]{0,1:T(8,128)(2,1)S(1)} %bitcast.93), channel_id=1, replica_groups=mesh['dp'=2,'row'=4,'col'=4] {'col'}, dimensions={0}, use_global_device_ids=true | all-gather | bytes 327680 | tf_op jit(solution)/shard_map/all_gather | solution.py:148
  93.8 6.2 %collective-permute-done = bf16[128,256]{0,1:T(8,128)(2,1)S(1)} collective-permute-done((bf16[128,256]{0,1:T(8,128)(2,1)S(1)}, bf16[128,256]{0,1:T(8,128)(2,1)S(1)}, u32[]{:S(2)}, u32[]{:S(2)}) %collective-permute-start) | collective-permute-done | bytes 65568 | tf_op jit(solution)/shard_map/ppermute | solution.py:20
  100.0 3.8 collective-permute-start.2
  103.8 2.3 collective-permute-done.1
  109.7 1.1 fusion.40
  110.9 5.8 %all_gather.22 = bf16[512,256]{1,0:T(8,128)(2,1)S(1)} all-gather(bf16[128,256]{1,0:T(8,128)(2,1)S(1)} %copy-done.29), channel_id=1, replica_groups=mesh['dp'=2,'row'=4,'col'=4] {'row'}, dimensions={0}, use_global_device_ids=true | all-gather | bytes 327680 | tf_op jit(solution)/shard_map/all_gather | solution.py:73
  116.7 1.8 fusion.78
  118.6 13.6 %reduce-scatter.13.cloned.1.call-done = f32[128,256]{1,0:T(8,128)} async-done(((f32[512,256]{1,0:T(8,128)}), f32[128,256]{1,0:T(8,128)}) %reduce-scatter.13.cloned.1.call-update) | async-done | bytes 131088 | tf_op jit(solution)/shard_map/reduce_scatter | solution.py:97
  132.2 1.0 fusion.68
  133.2 11.8 %all-reduce.4 = (f32[128]{0:T(128)S(1)}, f32[128]{0:T(128)S(1)}) all-reduce(f32[128]{0:T(128)S(1)} %get-tuple-element.84, f32[128]{0:T(128)S(1)} %get-tuple-element.83), channel_id=1, replica_groups=mesh['dp'=2,'row'=4,'col'=4] {'col'}, use_global_device_ids=true, to_apply=%region_10.11 | all-reduce | flops 256 | bytes 2048 | tf_op jit(solution)/shard_map/psum | solution.py:38
  145.6 5.8 %all_gather.21 = bf16[512,256]{1,0:T(8,128)(2,1)S(1)} all-gather(bf16[128,256]{1,0:T(8,128)(2,1)S(1)} %add_convert_fusion.1), channel_id=1, replica_groups=mesh['dp'=2,'row'=4,'col'=4] {'row'}, dimensions={0}, use_global_device_ids=true | all-gather | bytes 327680 | tf_op jit(solution)/shard_map/all_gather | solution.py:73
  151.4 1.7 fusion.76
  153.3 24.9 %reduce-scatter.19.cloned.1.call-done = f32[128,1024]{1,0:T(8,128)} async-done(((f32[512,1024]{1,0:T(8,128)}), f32[128,1024]{1,0:T(8,128)}) %reduce-scatter.19.cloned.1.call-update) | async-done | bytes 524304 | tf_op jit(solution)/shard_map/reduce_scatter | solution.py:86
  178.2 44.9 %reduce-scatter.15.cloned.1.call-done = f32[128,1024]{1,0:T(8,128)} async-done(((f32[512,1024]{1,0:T(8,128)}), f32[128,1024]{1,0:T(8,128)}) %reduce-scatter.15.cloned.1.call-update) | async-done | bytes 524304 | tf_op jit(solution)/shard_map/reduce_scatter | solution.py:86
  223.1 2.3 fusion.69
  226.1 3.2 collective-permute-start.8
  229.2 7.2 %collective-permute-done.6 = bf16[128,1024]{1,0:T(8,128)(2,1)S(1)} collective-permute-done((bf16[128,1024]{1,0:T(8,128)(2,1)S(1)}, bf16[128,1024]{1,0:T(8,128)(2,1)S(1)}, u32[]{:S(2)}, u32[]{:S(2)}) %collective-permute-start.6) | collective-permute-done | bytes 262176 | tf_op jit(solution)/shard_map/ppermute | solution.py:20
  236.4 2.0 collective-permute-start.7
  238.4 3.0 collective-permute-start.3
  241.4 6.2 %collective-permute-done.7 = bf16[128,1024]{1,0:T(8,128)(2,1)S(1)} collective-permute-done((bf16[128,1024]{1,0:T(8,128)(2,1)S(1)}, bf16[128,1024]{1,0:T(8,128)(2,1)S(1)}, u32[]{:S(2)}, u32[]{:S(2)}) %collective-permute-start.7) | collective-permute-done | bytes 262176 | tf_op jit(solution)/shard_map/ppermute | solution.py:20
  247.6 4.2 fusion.10
  251.8 1.3 fusion.79
  253.1 1.9 collective-permute-start.5
  255.2 9.1 %collective-permute-done.5 = bf16[128,1024]{1,0:T(8,128)(2,1)S(1)} collective-permute-done((bf16[128,1024]{1,0:T(8,128)(2,1)}, bf16[128,1024]{1,0:T(8,128)(2,1)S(1)}, u32[]{:S(2)}, u32[]{:S(2)}) %collective-permute-start.5) | collective-permute-done | bytes 262176 | tf_op jit(solution)/shard_map/ppermute | solution.py:22
  264.4 4.3 fusion.17
  269.6 1.2 fusion.77
  270.9 3.2 reduce-scatter.21.cloned.1.call-done
  274.1 1.7 multiply_reduce_fusion
  275.8 11.7 %all-reduce.3 = (f32[128]{0:T(128)S(1)}, f32[128]{0:T(128)S(1)}) all-reduce(f32[128]{0:T(128)S(1)} %get-tuple-element.64, f32[128]{0:T(128)S(1)} %get-tuple-element.80), channel_id=1, replica_groups=mesh['dp'=2,'row'=4,'col'=4] {'col'}, use_global_device_ids=true, to_apply=%region_18.20 | all-reduce | flops 256 | bytes 2048 | tf_op jit(solution)/shard_map/psum | solution.py:38
  287.5 11.3 %reduce-scatter.17.cloned.1.call-done = f32[128,256]{1,0:T(8,128)} async-done(((f32[512,256]{1,0:T(8,128)}), f32[128,256]{1,0:T(8,128)}) %reduce-scatter.17.cloned.1.call-update) | async-done | bytes 131088 | tf_op jit(solution)/shard_map/reduce_scatter | solution.py:97
  298.7 2.3 fusion.71
  301.7 5.8 %all_gather.23 = bf16[512,256]{1,0:T(8,128)(2,1)S(1)} all-gather(bf16[128,256]{1,0:T(8,128)(2,1)S(1)} %convert_element_type.98), channel_id=1, replica_groups=mesh['dp'=2,'row'=4,'col'=4] {'row'}, dimensions={0}, use_global_device_ids=true | all-gather | bytes 327680 | tf_op jit(solution)/shard_map/all_gather | solution.py:73
  307.5 2.0 fusion.80
  309.6 21.9 %reduce-scatter.23.cloned.1.call-done = f32[128,256]{1,0:T(8,128)} async-done(((f32[512,256]{1,0:T(8,128)}), f32[128,256]{1,0:T(8,128)}) %reduce-scatter.23.cloned.1.call-update) | async-done | bytes 131088 | tf_op jit(solution)/shard_map/reduce_scatter | solution.py:86
  332.7 1.3 fusion.3
  334.0 2.0 convolution_multiply_fusion.1
  336.1 1.2 fusion.32
  337.3 1.9 fusion.74
  339.2 17.0 %reduce-scatter.25.cloned.1.call-done = f32[128,256]{0,1:T(8,128)} async-done(((f32[512,256]{0,1:T(8,128)}), f32[128,256]{0,1:T(8,128)}) %reduce-scatter.25.cloned.1.call-update) | async-done | bytes 131088 | tf_op jit(solution)/shard_map/reduce_scatter | solution.py:231
  357.2 22.1 %reduce-scatter.27.cloned.1.call-done = f32[128,256]{0,1:T(8,128)} async-done(((f32[512,256]{0,1:T(8,128)}), f32[128,256]{0,1:T(8,128)}) %reduce-scatter.27.cloned.1.call-update) | async-done | bytes 131088 | tf_op jit(solution)/shard_map/reduce_scatter | solution.py:232
  380.3 7.6 %collective-permute-done.9 = bf16[128,768]{0,1:T(8,128)(2,1)S(1)} collective-permute-done((bf16[128,768]{0,1:T(8,128)(2,1)S(1)}, bf16[128,768]{0,1:T(8,128)(2,1)S(1)}, u32[]{:S(2)}, u32[]{:S(2)}) %collective-permute-start.9) | collective-permute-done | bytes 196640 | tf_op jit(solution)/shard_map/ppermute | solution.py:20
  387.9 3.8 collective-permute-start.11
  391.7 3.9 collective-permute-done.10
  396.7 1.2 copy-done.11
  397.8 1.2 fusion.24
  399.2 1.4 fusion.82
  400.6 1.4 fusion.81
  403.0 1.3 fusion.22
  404.6 21.9 %all-reduce = (f32[512]{0:T(512)}, f32[1024]{0:T(1024)}) all-reduce(f32[512]{0:T(512)S(1)} %reshape.258, f32[1024]{0:T(1024)S(1)} %get-tuple-element.107), channel_id=1, replica_groups=mesh['dp'=2,'row'=4,'col'=4] {'dp','col'}, use_global_device_ids=true, to_apply=%region_34.36 | all-reduce | flops 1536 | bytes 12288 | tf_op jit(solution)/shard_map/psum | solution.py:259
  426.5 1.1 fusion.53
  427.6 8.4 %all-reduce.2 = (f32[128]{0:T(128)S(1)}, f32[128]{0:T(128)S(1)}) all-reduce(f32[128]{0:T(128)S(1)} %get-tuple-element.66, f32[128]{0:T(128)S(1)} %get-tuple-element.67), channel_id=1, replica_groups=mesh['dp'=2,'row'=4,'col'=4] {'col'}, use_global_device_ids=true, to_apply=%region_27.29 | all-reduce | flops 256 | bytes 2048 | tf_op jit(solution)/shard_map/psum | solution.py:38
  436.0 13.0 %all-reduce.1 = (f32[256]{0:T(256)}, f32[256]{0:T(256)}, f32[256]{0:T(256)}, f32[256]{0:T(256)}, f32[256]{0:T(256)}, /*index=5*/f32[256]{0:T(256)}) all-reduce(f32[256]{0:T(256)S(1)} %get-tuple-element.65, f32[256]{0:T(256)S(1)} %get-tuple-element.82, f32[256]{0:T(256)S(1)} %copy-done.42, ...), channel_id=1, replica_groups=mesh['dp'=2,'row'=4,'col'=4] {'dp','row'}, use_global_device_ids=true, to_apply=%region_29.31 | all-reduce | flops 1536 | bytes 12288 | tf_op jit(solution)/shard_map/psum | solution.py:248
  449.0 1.7 fusion.52
  450.7 60.4 %all-reduce.9.cloned.1.call-done = (f32[256,768]{1,0:T(8,128)}, f32[256,256]{1,0:T(8,128)}, f32[256,1024]{1,0:T(8,128)}, f32[1024,256]{1,0:T(8,128)}) async-done(((f32[256,768]{1,0:T(8,128)}, f32[256,256]{1,0:T(8,128)}, f32[256,1024]{1,0:T(8,128)}, f32[1024,256]{1,0:T(8,128)}), (f32[256,768]{1,0:T(8,128)}, f32[256,256]{1,0:T(8,128)}, f32[256,1024]{1,0:T(8,128)}, ...) | async-done | bytes 3145744 | tf_op jit(solution)/shard_map/psum | solution.py:245
  511.1 2.2 copy.60
  513.3 1.7 copy.61
  515.0 1.0 copy.62
  (178 shorter events, 16.1 us)
Async XLA Ops:
  7.2 144.2 %copy-start = (bf16[256,1024]{1,0:T(8,128)(2,1)S(1)}, bf16[256,1024]{1,0:T(8,128)(2,1)}, u32[]{:S(2)}) copy-start(bf16[256,1024]{1,0:T(8,128)(2,1)} %param.26) | copy-start | bytes 1572868
  7.2 57.7 %reduce-scatter.11.cloned.1.call-start = ((), (), s32[]{:S(2)}) async-start(), calls=%async_computation.10 | async-start | bytes 1966080 | tf_op jit(solution)/shard_map/reduce_scatter | solution.py:86
  22.7 8.4 %copy-start.44 = (f32[512]{0:T(512)S(1)}, f32[512]{0:T(512)}, u32[]{:S(2)}) copy-start(f32[512]{0:T(512)} %param.21) | copy-start | bytes 6148
  31.1 101.1 %reduce-scatter.13.cloned.1.call-start = ((), (), s32[]{:S(2)}) async-start(), calls=%async_computation.11 | async-start | bytes 655360 | tf_op jit(solution)/shard_map/reduce_scatter | solution.py:97
  31.2 62.1 %copy-start.37 = (f32[4,1,64]{2,1,0:T(1,128)}, f32[4,1,64]{2,1,0:T(1,128)S(1)}, u32[]{:S(2)}) copy-start(f32[4,1,64]{2,1,0:T(1,128)S(1)} %get-tuple-element.115) | copy-start | bytes 3076
  66.0 44.8 %copy-start.16 = (f32[128,768]{0,1:T(8,128)}, f32[128,768]{0,1:T(8,128)S(1)}, u32[]{:S(2)}) copy-start(f32[128,768]{0,1:T(8,128)S(1)} %copy.38) | copy-start | bytes 1179652
  79.6 13.8 %copy-start.9 = (bf16[512,256]{0,1:T(8,128)(2,1)}, bf16[512,256]{0,1:T(8,128)(2,1)S(1)}, u32[]{:S(2)}) copy-start(bf16[512,256]{0,1:T(8,128)(2,1)S(1)} %all_gather.19) | copy-start | bytes 786436
  92.7 17.0 %copy-start.26 = (bf16[256,256]{1,0:T(8,128)(2,1)S(1)}, bf16[256,256]{1,0:T(8,128)(2,1)}, u32[]{:S(2)}) copy-start(bf16[256,256]{1,0:T(8,128)(2,1)} %param.22) | copy-start | bytes 393220
  93.3 23.3 %copy-start.35 = (f32[4,128]{1,0:T(4,128)}, f32[4,128]{1,0:T(4,128)S(1)}, u32[]{:S(2)}) copy-start(f32[4,128]{1,0:T(4,128)S(1)} %get-tuple-element.121) | copy-start | bytes 6148
  93.4 17.5 %copy-start.29 = (bf16[128,256]{1,0:T(8,128)(2,1)S(1)}, bf16[128,256]{1,0:T(8,128)(2,1)}, u32[]{:S(2)}) copy-start(bf16[128,256]{1,0:T(8,128)(2,1)} %param.17) | copy-start | bytes 196612
  93.4 23.3 %copy-start.10 = (bf16[1024,256]{1,0:T(8,128)(2,1)S(1)}, bf16[1024,256]{1,0:T(8,128)(2,1)}, u32[]{:S(2)}) copy-start(bf16[1024,256]{1,0:T(8,128)(2,1)} %param.28) | copy-start | bytes 1572868
  93.7 24.8 %copy-start.22 = (bf16[128,4,64]{0,2,1:T(8,128)(2,1)}, bf16[128,4,64]{0,2,1:T(8,128)(2,1)S(1)}, u32[]{:S(2)}) copy-start(bf16[128,4,64]{0,2,1:T(8,128)(2,1)S(1)} %fusion.6) | copy-start | bytes 196612
  93.7 6.2 %collective-permute-start = (bf16[128,256]{0,1:T(8,128)(2,1)S(1)}, bf16[128,256]{0,1:T(8,128)(2,1)S(1)}, u32[]{:S(2)}, u32[]{:S(2)}) collective-permute-start(bf16[128,256]{0,1:T(8,128)(2,1)S(1)} %bitcast.86), channel_id=1, source_target_pairs={{0,1},{1,2},{2,3},{3,0},{4,5},{5,6},{6,7},{7,4},{8,9},{9,10},{10,1... | collective-permute-start | bytes 196616 | tf_op jit(solution)/shard_map/ppermute | solution.py:20
  100.0 3.8 copy-start.30
  100.0 6.2 %collective-permute-start.1 = (bf16[128,256]{0,1:T(8,128)(2,1)S(1)}, bf16[128,256]{0,1:T(8,128)(2,1)}, u32[]{:S(2)}, u32[]{:S(2)}) collective-permute-start(bf16[128,256]{0,1:T(8,128)(2,1)S(1)} %collective-permute-done), channel_id=1, source_target_pairs={{0,1},{1,2},{2,3},{3,0},{4,5},{5,6},{6,7},{7,4},{8,9},{9,10},{10,1... | collective-permute-start | bytes 196616 | tf_op jit(solution)/shard_map/ppermute | solution.py:20
  100.0 7.9 %collective-permute-start.2 = (bf16[128,256]{0,1:T(8,128)(2,1)S(1)}, bf16[128,256]{0,1:T(8,128)(2,1)S(1)}, u32[]{:S(2)}, u32[]{:S(2)}) collective-permute-start(bf16[128,256]{0,1:T(8,128)(2,1)S(1)} %bitcast.87), channel_id=1, source_target_pairs={{0,3},{1,0},{2,1},{3,2},{4,7},{5,4},{6,5},{7,6},{8,11},{9,8},{10,9... | collective-permute-start | bytes 196616 | tf_op jit(solution)/shard_map/ppermute | solution.py:22
  109.7 8.8 %copy-start.24 = (bf16[1024,256]{0,1:T(8,128)(2,1)}, bf16[1024,256]{0,1:T(8,128)(2,1)S(1)}, u32[]{:S(2)}) copy-start(bf16[1024,256]{0,1:T(8,128)(2,1)S(1)} %constant_dynamic-update-slice_fusion) | copy-start | bytes 1572868
  110.8 67.4 %reduce-scatter.19.cloned.1.call-start = ((), (), s32[]{:S(2)}) async-start(), calls=%async_computation.14 | async-start | bytes 2621440 | tf_op jit(solution)/shard_map/reduce_scatter | solution.py:86
  116.7 1.9 copy-start.5
  116.7 15.5 %copy-start.13 = (bf16[128,256]{1,0:T(8,128)(2,1)S(1)}, bf16[128,256]{1,0:T(8,128)(2,1)}, u32[]{:S(2)}) copy-start(bf16[128,256]{1,0:T(8,128)(2,1)} %param.16) | copy-start | bytes 196612
  116.7 15.5 %copy-start.45 = (f32[256]{0:T(256)S(1)}, f32[256]{0:T(256)}, u32[]{:S(2)}) copy-start(f32[256]{0:T(256)} %param.23) | copy-start | bytes 3076
  116.7 28.9 %copy-start.31 = (f32[256]{0:T(256)S(1)}, f32[256]{0:T(256)}, u32[]{:S(2)}) copy-start(f32[256]{0:T(256)} %param.24) | copy-start | bytes 3076
  116.7 28.8 %copy-start.46 = (f32[256]{0:T(256)S(1)}, f32[256]{0:T(256)}, u32[]{:S(2)}) copy-start(f32[256]{0:T(256)} %param.25) | copy-start | bytes 3076
  118.5 104.6 %reduce-scatter.15.cloned.1.call-start = ((), (), s32[]{:S(2)}) async-start(), calls=%async_computation.12 | async-start | bytes 2621440 | tf_op jit(solution)/shard_map/reduce_scatter | solution.py:86
  145.0 8.2 %copy-start.33 = (f32[128]{0:T(128)}, f32[128]{0:T(128)S(1)}, u32[]{:S(2)}) copy-start(f32[128]{0:T(128)S(1)} %get-tuple-element.117) | copy-start | bytes 1540
  151.4 1.8 copy-start.7
  151.4 71.7 %copy-start.39 = (f32[1024]{0:T(1024)S(1)}, f32[1024]{0:T(1024)}, u32[]{:S(2)}) copy-start(f32[1024]{0:T(1024)} %param.27) | copy-start | bytes 12292
  153.2 120.9 %reduce-scatter.21.cloned.1.call-start = ((), (), s32[]{:S(2)}) async-start(), calls=%async_computation.15 | async-start | bytes 655360 | tf_op jit(solution)/shard_map/reduce_scatter | solution.py:97
  225.4 11.0 %collective-permute-start.6 = (bf16[128,1024]{1,0:T(8,128)(2,1)S(1)}, bf16[128,1024]{1,0:T(8,128)(2,1)S(1)}, u32[]{:S(2)}, u32[]{:S(2)}) collective-permute-start(bf16[128,1024]{1,0:T(8,128)(2,1)S(1)} %get-tuple-element.108), channel_id=1, source_target_pairs={{0,1},{1,2},{2,3},{3,0},{4,5},{5,6},{6,7},{7,4},{8,9},{9,10},{10,1... | collective-permute-start | bytes 786440 | tf_op jit(solution)/shard_map/ppermute | solution.py:20
  226.1 15.3 %collective-permute-start.8 = (bf16[128,1024]{1,0:T(8,128)(2,1)S(1)}, bf16[128,1024]{1,0:T(8,128)(2,1)S(1)}, u32[]{:S(2)}, u32[]{:S(2)}) collective-permute-start(bf16[128,1024]{1,0:T(8,128)(2,1)S(1)} %get-tuple-element.108), channel_id=1, source_target_pairs={{0,3},{1,0},{2,1},{3,2},{4,7},{5,4},{6,5},{7,6},{8,11},{9,8},{10,9... | collective-permute-start | bytes 786440 | tf_op jit(solution)/shard_map/ppermute | solution.py:22
  236.4 11.2 %collective-permute-start.7 = (bf16[128,1024]{1,0:T(8,128)(2,1)S(1)}, bf16[128,1024]{1,0:T(8,128)(2,1)S(1)}, u32[]{:S(2)}, u32[]{:S(2)}) collective-permute-start(bf16[128,1024]{1,0:T(8,128)(2,1)S(1)} %collective-permute-done.6), channel_id=1, source_target_pairs={{0,1},{1,2},{2,3},{3,0},{4,5},{5,6},{6,7},{7,4},{8,9},{9,10},{10,1... | collective-permute-start | bytes 786440 | tf_op jit(solution)/shard_map/ppermute | solution.py:20
  238.4 16.6 %collective-permute-start.3 = (bf16[128,1024]{1,0:T(8,128)(2,1)}, bf16[128,1024]{1,0:T(8,128)(2,1)}, u32[]{:S(2)}, u32[]{:S(2)}) collective-permute-start(bf16[128,1024]{1,0:T(8,128)(2,1)} %get-tuple-element.112), channel_id=1, source_target_pairs={{0,1},{1,2},{2,3},{3,0},{4,5},{5,6},{6,7},{7,4},{8,9},{9,10},{10,1... | collective-permute-start | bytes 786440 | tf_op jit(solution)/shard_map/ppermute | solution.py:20
  253.1 45.6 %reduce-scatter.17.cloned.1.call-start = ((), (), s32[]{:S(2)}) async-start(), calls=%async_computation.13 | async-start | bytes 655360 | tf_op jit(solution)/shard_map/reduce_scatter | solution.py:97
  253.1 11.2 %collective-permute-start.5 = (bf16[128,1024]{1,0:T(8,128)(2,1)}, bf16[128,1024]{1,0:T(8,128)(2,1)S(1)}, u32[]{:S(2)}, u32[]{:S(2)}) collective-permute-start(bf16[128,1024]{1,0:T(8,128)(2,1)} %get-tuple-element.112), channel_id=1, source_target_pairs={{0,3},{1,0},{2,1},{3,2},{4,7},{5,4},{6,5},{7,6},{8,11},{9,8},{10,9... | collective-permute-start | bytes 786440 | tf_op jit(solution)/shard_map/ppermute | solution.py:22
  255.0 9.4 %collective-permute-start.4 = (bf16[128,1024]{1,0:T(8,128)(2,1)}, bf16[128,1024]{1,0:T(8,128)(2,1)S(1)}, u32[]{:S(2)}, u32[]{:S(2)}) collective-permute-start(bf16[128,1024]{1,0:T(8,128)(2,1)} %collective-permute-done.3), channel_id=1, source_target_pairs={{0,1},{1,2},{2,3},{3,0},{4,5},{5,6},{6,7},{7,4},{8,9},{9,10},{10,1... | collective-permute-start | bytes 786440 | tf_op jit(solution)/shard_map/ppermute | solution.py:20
  270.9 38.8 %copy-start.36 = (f32[4,128]{1,0:T(4,128)S(1)}, f32[4,128]{1,0:T(4,128)}, u32[]{:S(2)}) copy-start(f32[4,128]{1,0:T(4,128)} %copy-done.35) | copy-start | bytes 6148
  270.9 61.8 %copy-start.23 = (bf16[128,4,64]{0,2,1:T(8,128)(2,1)S(1)}, bf16[128,4,64]{0,2,1:T(8,128)(2,1)}, u32[]{:S(2)}) copy-start(bf16[128,4,64]{0,2,1:T(8,128)(2,1)} %copy-done.22) | copy-start | bytes 196612
  270.9 60.7 %reduce-scatter.23.cloned.1.call-start = ((), (), s32[]{:S(2)}) async-start(), calls=%async_computation.16 | async-start | bytes 655360 | tf_op jit(solution)/shard_map/reduce_scatter | solution.py:86
  301.7 32.3 %copy-start.38 = (f32[4,1,64]{2,1,0:T(1,128)S(1)}, f32[4,1,64]{2,1,0:T(1,128)}, u32[]{:S(2)}) copy-start(f32[4,1,64]{2,1,0:T(1,128)} %copy-done.37) | copy-start | bytes 3076
  307.5 25.2 %copy-start.3 = (bf16[512,256]{1,0:T(8,128)(2,1)}, bf16[512,256]{1,0:T(8,128)(2,1)S(1)}, u32[]{:S(2)}) copy-start(bf16[512,256]{1,0:T(8,128)(2,1)S(1)} %all_gather.23) | copy-start | bytes 786436
  309.6 46.7 %reduce-scatter.25.cloned.1.call-start = ((), (), s32[]{:S(2)}) async-start(), calls=%async_computation.17 | async-start | bytes 655360 | tf_op jit(solution)/shard_map/reduce_scatter | solution.py:231
  336.0 43.2 %reduce-scatter.27.cloned.1.call-start = ((), (), s32[]{:S(2)}) async-start(), calls=%async_computation.18 | async-start | bytes 655360 | tf_op jit(solution)/shard_map/reduce_scatter | solution.py:232
  337.3 89.3 %reduce-scatter.29.cloned.1.call-start = ((), (), s32[]{:S(2)}) async-start(), calls=%async_computation.19 | async-start | bytes 655360 | tf_op jit(solution)/shard_map/reduce_scatter | solution.py:97
  357.1 40.7 %copy-start.15 = (bf16[256,768]{1,0:T(8,128)(2,1)S(1)}, bf16[256,768]{1,0:T(8,128)(2,1)}, u32[]{:S(2)}) copy-start(bf16[256,768]{1,0:T(8,128)(2,1)} %param.20) | copy-start | bytes 1179652
  380.2 7.7 %collective-permute-start.9 = (bf16[128,768]{0,1:T(8,128)(2,1)S(1)}, bf16[128,768]{0,1:T(8,128)(2,1)S(1)}, u32[]{:S(2)}, u32[]{:S(2)}) collective-permute-start(bf16[128,768]{0,1:T(8,128)(2,1)S(1)} %bitcast.76), channel_id=1, source_target_pairs={{0,1},{1,2},{2,3},{3,0},{4,5},{5,6},{6,7},{7,4},{8,9},{9,10},{10,1... | collective-permute-start | bytes 589832 | tf_op jit(solution)/shard_map/ppermute | solution.py:20
  387.9 7.8 %collective-permute-start.10 = (bf16[128,768]{0,1:T(8,128)(2,1)S(1)}, bf16[128,768]{0,1:T(8,128)(2,1)S(1)}, u32[]{:S(2)}, u32[]{:S(2)}) collective-permute-start(bf16[128,768]{0,1:T(8,128)(2,1)S(1)} %collective-permute-done.9), channel_id=1, source_target_pairs={{0,1},{1,2},{2,3},{3,0},{4,5},{5,6},{6,7},{7,4},{8,9},{9,10},{10,1... | collective-permute-start | bytes 589832 | tf_op jit(solution)/shard_map/ppermute | solution.py:20
  387.9 8.4 %collective-permute-start.11 = (bf16[128,768]{0,1:T(8,128)(2,1)S(1)}, bf16[128,768]{0,1:T(8,128)(2,1)S(1)}, u32[]{:S(2)}, u32[]{:S(2)}) collective-permute-start(bf16[128,768]{0,1:T(8,128)(2,1)S(1)} %bitcast.77), channel_id=1, source_target_pairs={{0,3},{1,0},{2,1},{3,2},{4,7},{5,4},{6,5},{7,6},{8,11},{9,8},{10,9... | collective-permute-start | bytes 589832 | tf_op jit(solution)/shard_map/ppermute | solution.py:22
  395.9 3.3 copy-start.2
  395.9 3.3 copy-start.6
  399.1 3.0 copy-start.4
  399.1 112.0 %all-reduce.9.cloned.1.call-start = ((), (), s32[]{:S(2)}) async-start(), calls=%async_computation.20 | async-start | bytes 6291456 | tf_op jit(solution)/shard_map/psum | solution.py:245
  399.1 1.5 copy-start.8
  399.2 2.9 copy-start.25
  400.6 2.4 copy-start.12
  403.0 1.4 copy-start.28
  404.3 22.2 %copy-start.14 = (bf16[128,256]{1,0:T(8,128)(2,1)S(1)}, bf16[128,256]{1,0:T(8,128)(2,1)}, u32[]{:S(2)}) copy-start(bf16[128,256]{1,0:T(8,128)(2,1)} %param.16) | copy-start | bytes 196612
  404.3 22.2 %copy-start.32 = (f32[256]{0:T(256)S(1)}, f32[256]{0:T(256)}, u32[]{:S(2)}) copy-start(f32[256]{0:T(256)} %param.18) | copy-start | bytes 3076
  404.3 31.7 %copy-start.40 = (f32[256]{0:T(256)S(1)}, f32[256]{0:T(256)}, u32[]{:S(2)}) copy-start(f32[256]{0:T(256)} %get-tuple-element.63) | copy-start | bytes 3076
  404.3 31.7 %copy-start.41 = (f32[256]{0:T(256)S(1)}, f32[256]{0:T(256)}, u32[]{:S(2)}) copy-start(f32[256]{0:T(256)} %get-tuple-element.81) | copy-start | bytes 3076
  404.3 31.7 %copy-start.42 = (f32[256]{0:T(256)S(1)}, f32[256]{0:T(256)}, u32[]{:S(2)}) copy-start(f32[256]{0:T(256)} %get-tuple-element.109) | copy-start | bytes 3076
  404.3 31.7 %copy-start.43 = (f32[256]{0:T(256)S(1)}, f32[256]{0:T(256)}, u32[]{:S(2)}) copy-start(f32[256]{0:T(256)} %get-tuple-element.114) | copy-start | bytes 3076
  404.3 44.7 %copy-start.18 = (f32[128,256]{1,0:T(8,128)S(1)}, f32[128,256]{1,0:T(8,128)}, u32[]{:S(2)}) copy-start(f32[128,256]{1,0:T(8,128)} %copy-done.17) | copy-start | bytes 393220
  511.1 3.9 copy-start.20
  511.1 4.9 copy-start.19
  (6 other events, 5.7 us)
Sparse Core Ops, SparseCore 0:
  31.2 33.6 reduce-scatter.10
  110.9 21.1 reduce-scatter.12
  134.5 43.6 reduce-scatter.18
  180.3 42.7 reduce-scatter.14
  253.2 20.8 reduce-scatter.20
  277.0 21.6 reduce-scatter.16
  309.7 21.8 reduce-scatter.22
  336.1 20.0 reduce-scatter.24
  359.1 20.1 reduce-scatter.26
  399.2 22.0 reduce-scatter.28
  424.9 86.1 all-reduce.8
